TPU v7x, 32 devices: a whole 2x2x4 slice. The times are simulated.
32 devices in a mesh: seq: 8 (over z, x), head: 4 (over y, core).
Axes of the slice: x: 2, y: 2, z: 4, core: 2. Of those that a mesh axis runs over, the one named last changes fastest.
Arguments:
- queries: bfloat16 [6144, 8192], P('seq', 'head'), may hold values from -6 to 6
- key_rows: bfloat16 [6144, 8192], P('seq', 'head'), may hold values from -0.5 to 0.5
- value_rows: bfloat16 [6144, 8192], P('seq', 'head'), may hold values from -130 to 130
- log_decay: float32 [64, 6144], P('head', 'seq'), may hold values from -1 to 0
- norm_gain: float32 [8192], P('head'), may hold values from 0.1 to 1.9
- grad_out: bfloat16 [6144, 8192], P('seq', 'head'), may hold values from -13 to 13
Outputs:
- output: bfloat16 [6144, 8192], P('seq', 'head')
- grad_queries: bfloat16 [6144, 8192], P('seq', 'head')
- grad_keys: bfloat16 [6144, 8192], P('seq', 'head')
- grad_values: bfloat16 [6144, 8192], P('seq', 'head')
- grad_gain: float32 [8192], P('head')
All inputs are finite; a program needn't handle non-finite values.
Results may differ from a plain program's by a relative error of at most 0.01.
Values sent between devices are 32-bit elements; how exact they have to be, the bound alone decides.
A program may use at most 192 MiB of HBM per device.

v0:
```python
import jax
import jax.numpy as jnp
from jax import lax
from jax.sharding import PartitionSpec as P

DH = 128
HD = 8192


EPSILON = 1e-06


def prefix(part, axis, combine, identity, reverse):
    count = lax.axis_size(axis)
    place = lax.axis_index(axis)
    ahead = count - 1 - place if reverse else place
    gathered = jax.tree.map(lambda a: lax.all_gather(a, axis), part)
    state = jax.tree.map(lambda a, e: jnp.zeros_like(a) + jnp.asarray(e, a.dtype), part, identity)

    def one(step, state):
        source = count - 1 - step if reverse else step
        return combine(
            state, jax.tree.map(lambda a: lax.dynamic_index_in_dim(a, source, 0, False), gathered)
        )

    return lax.fori_loop(0, ahead, one, state)


def split_pair(operand):
    high = operand.astype(jnp.bfloat16)
    low = (operand - high.astype(jnp.float32)).astype(jnp.bfloat16)
    return (high, low)


def split_product(form, left, right):
    if left.dtype == jnp.float32:
        high, low = split_pair(left)
        return jnp.einsum(form, high, right, preferred_element_type=jnp.float32) + jnp.einsum(
            form, low, right, preferred_element_type=jnp.float32
        )
    if right.dtype == jnp.float32:
        high, low = split_pair(right)
        return jnp.einsum(form, left, high, preferred_element_type=jnp.float32) + jnp.einsum(
            form, left, low, preferred_element_type=jnp.float32
        )
    return jnp.einsum(form, left, right, preferred_element_type=jnp.float32)


def causal_decay(cumulative):
    length = cumulative.shape[-1]
    below_diag = jnp.arange(length)[:, None] >= jnp.arange(length)[None, :]
    spread = cumulative[..., :, None] - cumulative[..., None, :]
    return jnp.where(below_diag, jnp.exp(jnp.where(below_diag, spread, 0.0)), 0.0)


def split_heads(matrix):
    return matrix.reshape(matrix.shape[0], -1, DH).transpose(1, 0, 2)


def merge_heads(tensor):
    return tensor.transpose(1, 0, 2).reshape(tensor.shape[1], -1)


def affine_combine(earlier, later):
    return (earlier[0] * later[0], later[0][:, None, None] * earlier[1] + later[1])


def intra_forward(operands):
    q_head, k_head, v_head, cumul = operands
    decay_mask = causal_decay(cumul)
    scores = jnp.dot(q_head, k_head.T, preferred_element_type=jnp.float32)
    weights = (scores * decay_mask).astype(jnp.bfloat16)
    return jnp.dot(weights, v_head, preferred_element_type=jnp.float32)


def intra_backward(operands):
    q_head, k_head, v_head, grad_head, cumul = operands
    decay_mask = causal_decay(cumul)
    scores = jnp.dot(q_head, k_head.T, preferred_element_type=jnp.float32)
    weights = (scores * decay_mask).astype(jnp.bfloat16)
    grad_scores = jnp.dot(grad_head, v_head.T, preferred_element_type=jnp.float32)
    grad_weights = (grad_scores * decay_mask).astype(jnp.bfloat16)
    grad_q = jnp.dot(grad_weights, k_head, preferred_element_type=jnp.float32)
    grad_k = jnp.dot(grad_weights.T, q_head, preferred_element_type=jnp.float32)
    grad_v = jnp.dot(weights.T, grad_head, preferred_element_type=jnp.float32)
    return (grad_q, grad_k, grad_v)


def on_device(queries, key_rows, value_rows, log_decay, norm_gain, grad_out):
    q_heads = split_heads(queries)
    k_heads = split_heads(key_rows)
    v_heads = split_heads(value_rows)
    cumulative = jnp.cumsum(log_decay, axis=1)
    block_total = cumulative[:, -1]
    growth = jnp.exp(cumulative)[..., None]
    tail = jnp.exp(block_total[:, None] - cumulative)[..., None]
    decay_total = jnp.exp(block_total)
    local_state = split_product("htd,hte->hde", k_heads * tail, v_heads)
    identity = (jnp.ones_like(decay_total), jnp.zeros_like(local_state))
    state_in = prefix((decay_total, local_state), "seq", affine_combine, identity, False)[1]
    intra = lax.map(intra_forward, (q_heads, k_heads, v_heads, cumulative))
    attended = intra + growth * split_product("htd,hde->hte", q_heads, state_in)
    mixed = merge_heads(attended)
    scaled_grad = grad_out.astype(jnp.float32) * norm_gain[None, :]
    square_sum = lax.psum(jnp.sum(mixed * mixed, axis=1), "head")
    inverse = lax.rsqrt(square_sum / HD + EPSILON)
    normed = mixed * inverse[:, None]
    inner_sum = lax.psum(jnp.sum(scaled_grad * normed, axis=1), "head")
    center = inner_sum / HD
    output = (normed * norm_gain[None, :]).astype(jnp.bfloat16)
    gain_part = jnp.sum(grad_out.astype(jnp.float32) * normed, axis=0)
    grad_gain = lax.psum(gain_part, "seq")
    grad_mixed = (inverse[:, None] * (scaled_grad - normed * center[:, None])).astype(jnp.bfloat16)
    grad_heads = split_heads(grad_mixed)
    state_grad = split_product("htd,hte->hde", q_heads * growth, grad_heads)
    identity = (jnp.ones_like(decay_total), jnp.zeros_like(state_grad))
    state_after = prefix((decay_total, state_grad), "seq", affine_combine, identity, True)[1]
    intra_q, intra_k, intra_v = lax.map(
        intra_backward, (q_heads, k_heads, v_heads, grad_heads, cumulative)
    )
    grad_q = intra_q + growth * split_product("hte,hde->htd", grad_heads, state_in)
    grad_k = intra_k + tail * split_product("hse,hde->hsd", v_heads, state_after)
    grad_v = intra_v + tail * split_product("hsd,hde->hse", k_heads, state_after)
    return (
        output,
        merge_heads(grad_q).astype(jnp.bfloat16),
        merge_heads(grad_k).astype(jnp.bfloat16),
        merge_heads(grad_v).astype(jnp.bfloat16),
        grad_gain,
    )


def solution(mesh):
    in_specs = (
        P("seq", "head"),
        P("seq", "head"),
        P("seq", "head"),
        P("head", "seq"),
        P("head"),
        P("seq", "head"),
    )
    out_specs = (P("seq", "head"), P("seq", "head"), P("seq", "head"), P("seq", "head"), P("head"))
    return jax.shard_map(
        on_device, mesh=mesh, in_specs=in_specs, out_specs=out_specs, check_vma=False
    )
```

profile of v0, /device:TPU:0, one launch (start us, length us, event | category | flops | bytes accessed | tf_op | source)
XLA Modules:
  0.0 436.8 jit_solution(12516096848934879581)
XLA Ops:
  12.4 4.7 %copy.68 = bf16[768,2048]{0,1:T(8,128)(2,1)} copy(bf16[768,2048]{1,0:T(8,128)(2,1)} %param.16) | data formatting | bytes 6291456 | tf_op args[2]
  25.3 4.6 %copy.71 = bf16[16,768,128]{2,1,0:T(8,128)(2,1)} copy(bf16[16,768,128]{1,2,0:T(8,128)(2,1)} %bitcast.184) | data formatting | bytes 6291456 | tf_op jit(solution)/shard_map/while | solution.py:101
  38.1 24.4 %all-reduce = f32[128]{0:T(128)S(1)} all-reduce(f32[128]{0:T(128)S(1)} %dynamic-update-slice), channel_id=2, replica_groups=mesh['seq'=8,'head'=4] {'seq'}, use_global_device_ids=true, to_apply=%add | all-reduce | flops 128 | bytes 1024
  62.6 3.4 broadcast.34.clone2
  65.9 45.5 %while.50 = (s32[]{:T(128)}, f32[16,768,128]{1,2,0:T(8,128)}, bf16[16,768,128]{2,1,0:T(8,128)(2,1)}, bf16[16,768,128]{2,1,0:T(8,128)(2,1)}, f32[16,768]{1,0:T(8,...) while((s32[]{:T(128)}, f32[16,768,128]{1,2,0:T(8,128)}, bf16[16,768,128]{2,1,0:T(8,128)(2,1)}, ...), condition=%wide.region_3.4_spmd, body=%wide.region_2.3_spmd.sunk | while | flops 305528832 | bytes 999513 | solution.py:101
  111.4 38.8 %all-gather.6.cloned.1.call-done = f32[128,128,128]{2,1,0:T(8,128)} async-done(((f32[16,128,128]{2,1,0:T(8,128)}), f32[128,128,128]{2,1,0:T(8,128)}) %all-gather.6.cloned.1.call-update) | async-done | bytes 8388624 | tf_op jit(solution)/shard_map/all_gather | solution.py:17
  155.0 4.4 fusion.59
  159.4 6.6 %copy.79 = f32[768,2048]{1,0:T(8,128)} copy(f32[768,2048]{0,1:T(8,128)} %bitcast.193) | data formatting | bytes 12582912 | tf_op jit(solution)/shard_map/reshape | solution.py:61
  165.9 5.8 %psum.21 = f32[768]{0:T(1024)S(1)} all-reduce(f32[768]{0:T(1024)S(1)} %get-tuple-element.338), channel_id=1, replica_groups=mesh['seq'=8,'head'=4] {'head'}, use_global_device_ids=true, to_apply=%region_7.8 | all-reduce | flops 768 | bytes 6144 | tf_op jit(solution)/shard_map/psum | solution.py:105
  171.8 4.8 %fusion.56 = (f32[2048]{0:T(1024)S(1)}, f32[768]{0:T(1024)S(1)}) fusion(bf16[768,2048]{1,0:T(8,128)(2,1)} %param.19, f32[768,2048]{1,0:T(8,128)} %copy.79, f32[768]{0:T(1024)S(1)} %add_rsqrt_fusion, f32[2048]{0:T(1024)S(1)} %copy-done.11), kind=kLoop, calls=%fused_computation.62 | loop fusion | flops 11007232 | bytes 9459712 | tf_op jit(solution)/shard_map/reduce_sum | solution.py:111
  176.6 6.4 %psum.22 = f32[768]{0:T(1024)S(1)} all-reduce(f32[768]{0:T(1024)S(1)} %get-tuple-element.281), channel_id=1, replica_groups=mesh['seq'=8,'head'=4] {'head'}, use_global_device_ids=true, to_apply=%region_9.10 | all-reduce | flops 768 | bytes 6144 | tf_op jit(solution)/shard_map/psum | solution.py:108
  183.0 5.9 %fusion.68 = (bf16[96,16,8,128]{3,2,1,0:T(8,128)(2,1)S(1)}, bf16[768,2048]{1,0:T(8,128)(2,1)}) fusion(f32[768,2048]{1,0:T(8,128)} %copy.79, bf16[768,2048]{1,0:T(8,128)(2,1)} %param.19, f32[768]{0:T(1024)S(1)} %broadcast_multiply_fusion, f32[2048]{0:T(1024)S(1)} %copy-done.11, f32[768]{0:T(1024)S(1)} %add_rsqrt_fusion), kind=kLoop, calls=%fused_computation.82 | loop fusion | flops 14155776 | bytes 15742976
  191.5 3.7 fusion.79
  201.8 3.3 broadcast.34.clone2.1
  208.3 137.7 %while.52 = (s32[]{:T(128)}, f32[16,768,128]{1,2,0:T(8,128)}, f32[16,768,128]{1,2,0:T(8,128)}, f32[16,768,128]{1,2,0:T(8,128)}, bf16[16,768,128]{2,1,0:T(8,128)(...) while((s32[]{:T(128)}, f32[16,768,128]{1,2,0:T(8,128)}, ...), condition=%wide.region_11.12_spmd, body=%wide.region_10.11_spmd.sunk | while | flops 762052608 | bytes 6122609 | solution.py:118
  346.1 8.5 %add_convert_fusion = bf16[16,768,128]{1,2,0:T(8,128)(2,1)} fusion(f32[16,768,128]{1,2,0:T(8,128)} %get-tuple-element.216, f32[16,768,128]{1,2,0:T(8,128)} %fusion.79, f32[16,768]{1,0:T(8,128)S(1)} %get-tuple-element.336, f32[16,128,128]{2,1,0:T(8,128)S(1)} %get-tuple-element.215, bf16[96,16,8,128]{3,2,1,0:T(8,128)(2,1)} %copy-done.9), kind=kOutput, calls=%fused_computation.73 | convolution fusion | flops 409993216 | bytes 19972096 | tf_op jit(solution)/shard_map/hte,hde->htd/dot_general | solution.py:43
  354.6 4.6 %copy.93 = bf16[768,2048]{1,0:T(8,128)(2,1)} copy(bf16[768,2048]{0,1:T(8,128)(2,1)} %bitcast.194) | data formatting | bytes 6291456
  359.2 30.1 %psum.23 = f32[2048]{0:T(1024)} all-reduce(f32[2048]{0:T(1024)S(1)} %get-tuple-element.280), channel_id=1, replica_groups=mesh['seq'=8,'head'=4] {'seq'}, use_global_device_ids=true, to_apply=%region_15.16 | all-reduce | flops 2048 | bytes 16384 | tf_op jit(solution)/shard_map/psum | solution.py:112
  389.4 10.7 %while.53 = (s32[]{:T(128)}, f32[16,128,128]{2,1,0:T(8,128)S(1)}, s32[]{:T(128)}, f32[8,16]{1,0:T(8,128)S(1)}, f32[8,16,128,128]{3,2,1,0:T(8,128)}, /*index=5*/s32[]{:T(128)}, s32[]{:T(128)}, s32[]{:T(128)}, s32[]{:T(128)}) while((s32[]{:T(128)}, f32[16,128,128]{2,1,0:T(8,128)S(1)}, s32[]{:T(128)}, f32[8,16]{1,0:T(8,128)S(1)}, ...), condition=%wide.region_13.14_spmd, body=%wide.region_12.13_spmd.sunk | while | flops 524294 | bytes 3146075 | solution.py:26
  403.1 3.7 fusion.75
  406.8 5.5 %fusion.58 = bf16[16,768,128]{1,2,0:T(8,128)(2,1)} fusion(f32[16,768,128]{1,2,0:T(8,128)} %get-tuple-element.217, f32[16,128,768]{2,1,0:T(8,128)S(1)} %fusion.77, f32[16,768]{1,0:T(8,128)S(1)} %get-tuple-element.337, bf16[16,768,128]{1,2,0:T(8,128)(2,1)S(1)} %bitcast.187, f32[16,128,128]{2,1,0:T(8,128)S(1)} %get-tuple-element.218), kind=kOutput, calls=%fused_computation.66 | convolution fusion | flops 409993216 | bytes 19972096 | tf_op jit(solution)/shard_map/hse,hde->hsd/dot_general | solution.py:43
  412.4 4.6 %copy.94 = bf16[768,2048]{1,0:T(8,128)(2,1)} copy(bf16[768,2048]{0,1:T(8,128)(2,1)} %bitcast.196) | data formatting | bytes 6291456
  417.0 8.3 %fusion.57 = bf16[16,768,128]{1,2,0:T(8,128)(2,1)} fusion(f32[16,768,128]{1,2,0:T(8,128)} %get-tuple-element.219, f32[16,128,768]{2,1,0:T(8,128)} %fusion.75, f32[16,768]{1,0:T(8,128)S(1)} %get-tuple-element.337, bf16[16,768,128]{1,2,0:T(8,128)(2,1)} %bitcast.181, f32[16,128,128]{2,1,0:T(8,128)S(1)} %get-tuple-element.218), kind=kOutput, calls=%fused_computation.64 | convolution fusion | flops 409993216 | bytes 19972096 | tf_op jit(solution)/shard_map/hsd,hde->hse/dot_general | solution.py:43
  425.3 4.6 %copy.95 = bf16[768,2048]{1,0:T(8,128)(2,1)} copy(bf16[768,2048]{0,1:T(8,128)(2,1)} %bitcast.195) | data formatting | bytes 6291456
  (186 shorter events, 234.3 us)
Async XLA Ops:
  7.2 3.3 copy-start
  7.2 143.0 %all-gather.6.cloned.1.call-start = ((), (), s32[]{:S(2)}) async-start(), calls=%async_computation | async-start | bytes 9437184 | tf_op jit(solution)/shard_map/all_gather | solution.py:17
  10.4 12.1 %copy-start.2 = (bf16[768,2048]{0,1:T(8,128)(2,1)}, bf16[768,2048]{0,1:T(8,128)(2,1)S(1)}, u32[]{:S(2)}) copy-start(bf16[768,2048]{0,1:T(8,128)(2,1)S(1)} %copy.65) | copy-start | bytes 9437188
  17.4 3.0 copy-start.4
  22.5 366.9 %all-gather.8.cloned.1.call-start = ((), (), s32[]{:S(2)}) async-start(), calls=%async_computation.1 | async-start | bytes 9437184 | tf_op jit(solution)/shard_map/all_gather | solution.py:17
  33.2 3.3 copy-start.6
  33.2 3.3 copy-start.12
  150.3 3.1 copy-start.7
  150.3 4.7 %copy-start.10 = (f32[16,768,128]{1,2,0:T(8,128)S(1)}, f32[16,768,128]{1,2,0:T(8,128)}, u32[]{:S(2)}) copy-start(f32[16,768,128]{1,2,0:T(8,128)} %get-tuple-element.214) | copy-start | bytes 18874372
  159.4 12.4 %copy-start.11 = (f32[2048]{0:T(1024)S(1)}, f32[2048]{0:T(1024)}, u32[]{:S(2)}) copy-start(f32[2048]{0:T(1024)} %param.18) | copy-start | bytes 24580
  188.9 7.4 %copy-start.9 = (bf16[96,16,8,128]{3,2,1,0:T(8,128)(2,1)}, bf16[96,16,8,128]{3,2,1,0:T(8,128)(2,1)S(1)}, u32[]{:S(2)}) copy-start(bf16[96,16,8,128]{3,2,1,0:T(8,128)(2,1)S(1)} %get-tuple-element.334) | copy-start | bytes 9437188
  191.5 3.7 copy-start.8
  400.1 3.0 copy-start.3
  403.1 3.7 copy-start.5
  425.3 4.6 %copy-start.1 = (f32[16,768]{1,0:T(8,128)S(1)}, f32[16,768]{1,0:T(8,128)}, u32[]{:S(2)}) copy-start(f32[16,768]{1,0:T(8,128)} %param.17) | copy-start | bytes 147460
Sparse Core Ops, SparseCore 0:
  22.6 127.5 all-gather.5
  198.7 132.5 all-gather.7
where the time goes:
time: 440 us; the launch traced here: 437 us
  matrix products  231 us (52%)
  blocking collectives  66.8 us (15%)
  local copies, waits for them, and re-layouts  61.9 us (14%)
  waiting for transfers between devices  38.8 us (9%)
  other arithmetic  22.7 us (5%)
  between operations  14.9 us (3%)
    dot_general x16, matrix products, intra_forward(): return jnp.dot(weights, v_head, preferred_element_type=jnp.float32)  45.1 us
    dot_general x16, matrix products, intra_backward(): grad_v = jnp.dot(weights.T, grad_head, preferred_element_type=jnp.float32)  44.1 us
    all_gather x2, waiting for transfers between devices, prefix(): gathered = jax.tree.map(lambda a: lax.all_gather(a, axis), part)  38.8 us
    dot_general x16, matrix products, intra_backward(): grad_q = jnp.dot(grad_weights, k_head, preferred_element_type=jnp.float32)  35.8 us
    dot_general x16, matrix products, intra_backward(): grad_k = jnp.dot(grad_weights.T, q_head, preferred_element_type=jnp.float32)  32.9 us
    psum x1, blocking collectives, on_device(): grad_gain = lax.psum(gain_part, 'seq')  30.1 us
    unnamed x35, local copies, waits for them, and re-layouts  27.5 us
    dot_general x4, matrix products, split_product(): jnp.einsum(form, left, low, preferred_element_type=jnp.float32)  26.7 us
  transfers between devices with their start and end apart: 2, of which 1 were waited for; matrix products, arithmetic and copies ran while one was open for 51% of the time, Pallas kernels for 0%

commit v1 on v0

v1 whole, which is shorter than its diff:
```python
import functools

import jax
import jax.numpy as jnp
from jax import lax
from jax.experimental import pallas as pl
from jax.experimental.pallas import tpu as pltpu
from jax.sharding import PartitionSpec as P

DH = 128
EPSILON = 1e-06
CHUNK = 256
F32 = jnp.float32
BF16 = jnp.bfloat16
MESH = pl.DeviceIdType.MESH
HIGHEST = lax.Precision.HIGHEST


def mm(left, right, dims):
    return lax.dot_general(left, right, (dims, ((), ())), preferred_element_type=F32)


AB = ((1,), (0,))
ABT = ((1,), (1,))
ATB = ((0,), (0,))


def chunk_cumsum(ld_ref, cum_ref, chunk):
    below = lax.broadcasted_iota(jnp.int32, (chunk, chunk), 0)
    right = lax.broadcasted_iota(jnp.int32, (chunk, chunk), 1)
    tri = (below <= right).astype(F32)
    for j in range(ld_ref.shape[1] // chunk):
        span = slice(j * chunk, (j + 1) * chunk)
        cum_ref[:, span] = lax.dot_general(
            ld_ref[:, span], tri, (AB, ((), ())), precision=HIGHEST, preferred_element_type=F32
        )


def cum_forms(cum_ref, h, j, chunk):
    row = cum_ref[pl.ds(h, 1), j * chunk : (j + 1) * chunk]
    column = jnp.broadcast_to(row, (DH, chunk)).T
    return row, column


def decay_of(row, column):
    chunk = row.shape[1]
    wide = jnp.concatenate([column] * (chunk // DH), axis=1)
    t = lax.broadcasted_iota(jnp.int32, (chunk, chunk), 0)
    s = lax.broadcasted_iota(jnp.int32, (chunk, chunk), 1)
    return jnp.where(t >= s, jnp.exp(wide - row), 0.0)


def remote(src, dst, send, recv, axis, target):
    return pltpu.make_async_remote_copy(
        src_ref=src, dst_ref=dst, send_sem=send, recv_sem=recv,
        device_id={axis: target}, device_id_type=MESH,
    )


def loop(count, body):
    lax.fori_loop(0, count, lambda i, c: (body(i), c)[1], 0)


class Chain:
    def __init__(self, n, reverse, bufs):
        (self.lsend, self.lrecv, self.zsend, self.zrecv, self.xsend, self.xrecv, self.sems) = bufs
        me = lax.axis_index("seq")
        self.partner = me + 1 - 2 * lax.rem(me, 2)
        place = n - 1 - me if reverse else me
        self.later = lax.rem(place, 2)
        self.row = place // 2
        self.first = self.row == 0
        self.last = self.row == n // 2 - 1
        step = -2 if reverse else 2
        self.next = lax.rem(me + step + n, n)

    def leads(self, h):
        return lax.rem(h, 2) != self.later

    def copy_l(self, h):
        return remote(self.lsend.at[h], self.lrecv.at[h], self.sems.at[0, h], self.sems.at[1, h], "seq", self.partner)

    def copy_x(self, h):
        return remote(self.xsend.at[h], self.xrecv.at[h], self.sems.at[2, h], self.sems.at[3, h], "seq", self.partner)

    def copy_z(self, h):
        return remote(self.zsend.at[h], self.zrecv.at[h], self.sems.at[4, h], self.sems.at[5, h], "seq", self.next)

    def start(self):
        @pl.when(self.first)
        def _():
            self.zrecv[...] = jnp.zeros_like(self.zrecv)

    def give(self, h, state, decay):
        self.lsend[h, 0:DH] = state
        self.lsend[h, DH : DH + 8] = jnp.broadcast_to(decay, (8, DH))

        @pl.when(jnp.logical_not(self.leads(h)))
        def _():
            self.copy_l(h).start()

    def step(self, h, state_in):
        @pl.when(self.leads(h))
        def _():
            self.copy_l(h).wait_recv()

            @pl.when(jnp.logical_not(self.first))
            def _():
                self.copy_z(h).wait_recv()

            state = self.zrecv[h]

            @pl.when(self.later == 1)
            def _():
                mid = self.lrecv[h, DH : DH + 1] * state + self.lrecv[h, 0:DH]
                self.xsend[h] = state
                self.copy_x(h).start()
                self.zsend[h] = self.lsend[h, DH : DH + 1] * mid + self.lsend[h, 0:DH]
                state_in[h] = mid

            @pl.when(self.later == 0)
            def _():
                mid = self.lsend[h, DH : DH + 1] * state + self.lsend[h, 0:DH]
                self.xsend[h] = mid
                self.copy_x(h).start()
                self.zsend[h] = self.lrecv[h, DH : DH + 1] * mid + self.lrecv[h, 0:DH]
                state_in[h] = state

            @pl.when(jnp.logical_not(self.last))
            def _():
                self.copy_z(h).start()

    def take(self, h, state_in):
        @pl.when(jnp.logical_not(self.leads(h)))
        def _():
            self.copy_x(h).wait_recv()
            state_in[h] = self.xrecv[h]

    def finish(self, h):
        @pl.when(self.leads(h))
        def _():
            self.copy_x(h).wait_send()

            @pl.when(jnp.logical_not(self.last))
            def _():
                self.copy_z(h).wait_send()

        @pl.when(jnp.logical_not(self.leads(h)))
        def _():
            self.copy_l(h).wait_send()


def main_kernel(
    n, peers, chunk,
    q_hbm, k_hbm, v_hbm, g_hbm, ld_ref, gain_ref,
    grad_hbm, out_hbm, s_out, r_out, gg_out,
    q, k, v, g, att, obuf, cum_ref, lc, state_in, sq_acc, in_acc,
    stat_send, stat_recv, gain_send, gain_recv, inv_b, cen_b,
    lsend1, lrecv1, zsend1, zrecv1, xsend1, xrecv1,
    lsend2, lrecv2, zsend2, zrecv2, xsend2, xrecv2,
    load_sem, store_sem, chain1_sem, chain2_sem, stat_sem, gain_sem,
):
    heads, tokens, _ = q.shape
    chunks = tokens // chunk
    me = lax.axis_index("seq")
    my_head = lax.axis_index("head")
    columns = heads * DH * peers

    def load(i, hbm, vmem, h):
        where = pl.ds(pl.multiple_of(h * DH, DH), DH)
        return pltpu.make_async_copy(hbm.at[:, where], vmem.at[h], load_sem.at[i, h])

    def store(i, vmem, hbm, h):
        where = pl.ds(pl.multiple_of(h * DH, DH), DH)
        return pltpu.make_async_copy(vmem.at[h], hbm.at[:, where], store_sem.at[i, h])

    def load_kv(h):
        load(0, k_hbm, k, h).start()
        load(1, v_hbm, v, h).start()

    def load_q(h):
        load(2, q_hbm, q, h).start()

    def load_g(h):
        load(3, g_hbm, g, h).start()

    loop(heads, load_kv)
    loop(heads, load_q)
    loop(heads, load_g)

    barrier = pltpu.get_barrier_semaphore()
    for off in range(1, n):
        pl.semaphore_signal(barrier, inc=1, device_id={"seq": lax.rem(me + off, n)}, device_id_type=MESH)
    for off in range(1, peers):
        pl.semaphore_signal(barrier, inc=1, device_id={"head": lax.rem(my_head + off, peers)}, device_id_type=MESH)
    chunk_cumsum(ld_ref, cum_ref, chunk)
    forward = Chain(n, False, (lsend1, lrecv1, zsend1, zrecv1, xsend1, xrecv1, chain1_sem))
    backward = Chain(n, True, (lsend2, lrecv2, zsend2, zrecv2, xsend2, xrecv2, chain2_sem))
    forward.start()
    backward.start()
    pl.semaphore_wait(barrier, n - 1 + peers - 1)

    def local_state(h):
        load(0, k_hbm, k, h).wait()
        load(1, v_hbm, v, h).wait()
        state = None
        for j in range(chunks):
            span = slice(j * chunk, (j + 1) * chunk)
            _, column = cum_forms(cum_ref, h, j, chunk)
            total = column[chunk - 1 : chunk, :]
            tail = jnp.exp(total - column)
            part = mm((k[h, span].astype(F32) * tail).astype(BF16), v[h, span], ATB)
            lc[h, j] = part
            state = part if j == 0 else jnp.exp(total) * state + part
            decay = total if j == 0 else decay + total
        forward.give(h, state, jnp.exp(decay))

    loop(heads, local_state)

    def intra(h):
        load(2, q_hbm, q, h).wait()
        for j in range(chunks):
            span = slice(j * chunk, (j + 1) * chunk)
            row, column = cum_forms(cum_ref, h, j, chunk)
            scores = mm(q[h, span], k[h, span], ABT)
            weights = (scores * decay_of(row, column)).astype(BF16)
            att[h, span] = mm(weights, v[h, span], AB)

    lag = forward.row * 2 + 1

    def overlap(i):
        @pl.when(i < heads)
        def _():
            intra(i)

        at = i - lag

        @pl.when(jnp.logical_and(at >= 0, at < heads))
        def _():
            forward.step(at, state_in)

    loop(heads + n, overlap)

    sq_acc[...] = jnp.zeros_like(sq_acc)
    in_acc[...] = jnp.zeros_like(in_acc)

    def inter(h):
        load(3, g_hbm, g, h).wait()
        forward.take(h, state_in)
        state = state_in[h]
        gain = gain_ref[pl.ds(h, 1), :]
        for j in range(chunks):
            span = slice(j * chunk, (j + 1) * chunk)
            _, column = cum_forms(cum_ref, h, j, chunk)
            rounded = state.astype(BF16)
            s_out[h, j] = rounded
            whole = att[h, span] + jnp.exp(column) * mm(q[h, span], rounded, AB)
            att[h, span] = whole
            sq_acc[span] += whole * whole
            in_acc[span] += g[h, span].astype(F32) * gain * whole
            if j < chunks - 1:
                state = jnp.exp(column[chunk - 1 : chunk, :]) * state + lc[h, j]

    loop(heads, inter)

    ones = jnp.ones((8, DH), F32)

    def row_sums(acc):
        return lax.dot_general(ones, acc, (ABT, ((), ())), precision=HIGHEST, preferred_element_type=F32)

    upper = lax.broadcasted_iota(jnp.int32, (8, tokens), 0) < 4
    stat_send[...] = jnp.where(upper, row_sums(sq_acc[...]), row_sums(in_acc[...]))

    def stat_copy(off, slot):
        return remote(stat_send, stat_recv.at[slot], stat_sem.at[0, off], stat_sem.at[1, off], "head", lax.rem(my_head + off, peers))

    for off in range(1, peers):
        stat_copy(off, my_head).start()
    stat_recv[my_head] = stat_send[...]
    for off in range(1, peers):
        stat_copy(off, lax.rem(my_head + peers - off, peers)).wait_recv()
    stats = stat_recv[0]
    for i in range(1, peers):
        stats = stats + stat_recv[i]
    inverse = lax.rsqrt(stats[0:1] / columns + EPSILON)
    center = stats[4:5] * inverse / columns
    inv_b[...] = jnp.broadcast_to(inverse, (DH, tokens)).T
    cen_b[...] = jnp.broadcast_to(center, (DH, tokens)).T

    def normalize(h):
        gain = gain_ref[pl.ds(h, 1), :]
        gain_part = jnp.zeros((1, DH), F32)
        state = None
        for j in reversed(range(chunks)):
            span = slice(j * chunk, (j + 1) * chunk)
            _, column = cum_forms(cum_ref, h, j, chunk)
            normed = att[h, span] * inv_b[span]
            obuf[h, span] = (normed * gain).astype(BF16)
            cotangent = g[h, span].astype(F32)
            gain_part = gain_part + jnp.sum(cotangent * normed, axis=0, keepdims=True)
            grad = (inv_b[span] * (cotangent * gain - normed * cen_b[span])).astype(BF16)
            g[h, span] = grad
            part = mm((q[h, span].astype(F32) * jnp.exp(column)).astype(BF16), grad, ATB)
            lc[h, j] = part
            total = column[chunk - 1 : chunk, :]
            state = part if state is None else jnp.exp(total) * state + part
            decay = total if j == chunks - 1 else decay + total
        backward.give(h, state, jnp.exp(decay))
        gain_send[pl.ds(h, 1), :] = gain_part
        store(0, g, grad_hbm, h).start()
        store(1, obuf, out_hbm, h).start()

    loop(heads, normalize)

    def gain_copy(off, slot):
        return remote(gain_send, gain_recv.at[slot], gain_sem.at[0, off], gain_sem.at[1, off], "seq", lax.rem(me + off, n))

    for off in range(1, n):
        gain_copy(off, me).start()
    gain_recv[me] = gain_send[...]

    loop(heads, lambda h: backward.step(h, state_in))

    def after(h):
        backward.take(h, state_in)
        state = state_in[h]
        for j in reversed(range(chunks)):
            r_out[h, j] = state.astype(BF16)
            if j > 0:
                _, column = cum_forms(cum_ref, h, j, chunk)
                state = jnp.exp(column[chunk - 1 : chunk, :]) * state + lc[h, j]

    loop(heads, after)

    for off in range(1, n):
        gain_copy(off, lax.rem(me + n - off, n)).wait_recv()
    gain_total = gain_recv[0]
    for i in range(1, n):
        gain_total = gain_total + gain_recv[i]
    gg_out[...] = gain_total

    def finish(h):
        forward.finish(h)
        backward.finish(h)
        store(0, g, grad_hbm, h).wait()
        store(1, obuf, out_hbm, h).wait()

    loop(heads, finish)
    for off in range(1, peers):
        stat_copy(off, my_head).wait_send()
    for off in range(1, n):
        gain_copy(off, me).wait_send()


def backward_kernel(
    chunk, q_ref, k_ref, v_ref, grad_ref, pass_ref, ld_ref, s_ref, r_ref,
    out_ref, gq_ref, gk_ref, gv_ref, cum_ref,
):
    h = pl.program_id(0)
    tokens = q_ref.shape[0]

    @pl.when(h == 0)
    def _():
        chunk_cumsum(ld_ref, cum_ref, chunk)

    out_ref[...] = pass_ref[...]
    for j in range(tokens // chunk):
        span = slice(j * chunk, (j + 1) * chunk)
        row, column = cum_forms(cum_ref, h, j, chunk)
        decay = decay_of(row, column)
        growth = jnp.exp(column)
        tail = jnp.exp(column[chunk - 1 : chunk, :] - column)
        q, k, v, grad = q_ref[span], k_ref[span], v_ref[span], grad_ref[span]
        weights = (mm(q, k, ABT) * decay).astype(BF16)
        grad_weights = (mm(grad, v, ABT) * decay).astype(BF16)
        state, after = s_ref[0, j], r_ref[0, j]
        gq_ref[span] = (mm(grad_weights, k, AB) + growth * mm(grad, state, ABT)).astype(BF16)
        gk_ref[span] = (mm(grad_weights, q, ATB) + tail * mm(v, after, ABT)).astype(BF16)
        gv_ref[span] = (mm(weights, grad, ATB) + tail * mm(k, after, AB)).astype(BF16)


def on_device(n, peers, queries, key_rows, value_rows, log_decay, norm_gain, grad_out):
    tokens, width = queries.shape
    heads = width // DH
    chunk = CHUNK if tokens % CHUNK == 0 else tokens
    chunks = tokens // chunk
    gain = norm_gain.reshape(heads, DH)
    anywhere = pl.BlockSpec(memory_space=pl.ANY)
    vmem = pl.BlockSpec(memory_space=pltpu.VMEM)
    rows = jax.ShapeDtypeStruct((tokens, width), BF16)
    states = jax.ShapeDtypeStruct((heads, chunks, DH, DH), BF16)
    per_head = lambda *shape, dtype=F32: pltpu.VMEM((heads, *shape), dtype)
    chain = [
        per_head(DH + 8, DH), per_head(DH + 8, DH), per_head(DH, DH),
        per_head(DH, DH), per_head(DH, DH), per_head(DH, DH),
    ]
    dma = pltpu.SemaphoreType.DMA
    grad, out, state, after, grad_gain = pl.pallas_call(
        functools.partial(main_kernel, n, peers, chunk),
        out_shape=(rows, rows, states, states, jax.ShapeDtypeStruct((heads, DH), F32)),
        in_specs=[anywhere] * 4 + [vmem] * 2,
        out_specs=(anywhere, anywhere, vmem, vmem, vmem),
        scratch_shapes=[
            per_head(tokens, DH, dtype=BF16), per_head(tokens, DH, dtype=BF16),
            per_head(tokens, DH, dtype=BF16), per_head(tokens, DH, dtype=BF16),
            per_head(tokens, DH), per_head(tokens, DH, dtype=BF16),
            pltpu.VMEM((heads, tokens), F32), per_head(chunks, DH, DH), per_head(DH, DH),
            pltpu.VMEM((tokens, DH), F32), pltpu.VMEM((tokens, DH), F32),
            pltpu.VMEM((8, tokens), F32), pltpu.VMEM((peers, 8, tokens), F32),
            pltpu.VMEM((heads, DH), F32), pltpu.VMEM((n, heads, DH), F32),
            pltpu.VMEM((tokens, DH), F32), pltpu.VMEM((tokens, DH), F32),
            *chain, *chain,
            dma((4, heads)), dma((2, heads)), dma((6, heads)), dma((6, heads)),
            dma((2, peers)), dma((2, n)),
        ],
        compiler_params=pltpu.CompilerParams(
            collective_id=0, has_side_effects=True, vmem_limit_bytes=60 * 1024 * 1024
        ),
        name="forward_chain",
    )(queries, key_rows, value_rows, grad_out, log_decay, gain)
    block = pl.BlockSpec((tokens, DH), lambda h: (0, h))
    per_state = pl.BlockSpec((1, chunks, DH, DH), lambda h: (h, 0, 0, 0))
    out, grad_q, grad_k, grad_v = pl.pallas_call(
        functools.partial(backward_kernel, chunk),
        grid=(heads,),
        out_shape=(rows,) * 4,
        in_specs=[block] * 5 + [pl.BlockSpec((heads, tokens), lambda h: (0, 0)), per_state, per_state],
        out_specs=(block,) * 4,
        scratch_shapes=[pltpu.VMEM((heads, tokens), F32)],
        name="backward_heads",
    )(queries, key_rows, value_rows, grad, out, log_decay, state, after)
    return out, grad_q, grad_k, grad_v, grad_gain.reshape(width)


def solution(mesh):
    in_specs = (
        P("seq", "head"),
        P("seq", "head"),
        P("seq", "head"),
        P("head", "seq"),
        P("head"),
        P("seq", "head"),
    )
    out_specs = (P("seq", "head"), P("seq", "head"), P("seq", "head"), P("seq", "head"), P("head"))
    return jax.shard_map(
        functools.partial(on_device, mesh.shape["seq"], mesh.shape["head"]),
        mesh=mesh, in_specs=in_specs, out_specs=out_specs, check_vma=False,
    )
```

time: 440 us -> 106 us (0.24)
  matrix products: 231 us -> 0 us
  Pallas kernels: 0 us -> 104 us
  blocking collectives: 66.8 us -> 0 us
  local copies, waits for them, and re-layouts: 61.9 us -> 0.61 us
  waiting for transfers between devices: 38.8 us -> 0 us
  other arithmetic: 22.7 us -> 0 us
  between operations: 14.9 us -> 0.66 us
    dot_general x92 -> x0, matrix products: 231 us -> none  [the longest x16 45.1 us: intra_forward(): return jnp.dot(weights, v_head, preferred_element_type=jnp.float32)]
    pallas_call x0 -> x2, Pallas kernels: none -> 104 us  [the longest x1 80.6 us: on_device(): pl.pallas_call(functools.partial(main_kernel, n, peers, chunk), out_shape...]
    psum x3 -> x0, blocking collectives: 42.4 us -> none  [the longest x1 30.1 us: on_device(): grad_gain = lax.psum(gain_part, 'seq')]
    all_gather x2 -> x0, waiting for transfers between devices: 38.8 us -> none  [prefix(): gathered = jax.tree.map(lambda a: lax.all_gather(a, axis), part)]
    unnamed x35 -> x3, local copies, waits for them, and re-layouts: 27.5 us -> 0.61 us
    unnamed x1 -> x0, blocking collectives: 24.4 us -> none
    another operation x6 -> x0, local copies, waits for them, and re-layouts: 13.3 us -> none
    while x3 -> x0, local copies, waits for them, and re-layouts: 10.7 us -> none  [on_device(): intra = lax.map(intra_forward, (q_heads, k_heads, v_heads, cumulative))]
  transfers between devices with their start and end apart: 2 -> 0, of which waited for: 1 -> 0; matrix products, arithmetic and copies ran while one was open for 51% -> 0% of each run, Pallas kernels for 0% -> 0%
where the time goes in v1:
time: 106 us; the launch traced here: 105 us
  Pallas kernels  104 us (98%)
    pallas_call x1, Pallas kernels, on_device(): pl.pallas_call(functools.partial(main_kernel, n, peers, chunk), out_shape...  80.6 us
    pallas_call x1, Pallas kernels, on_device(): pl.pallas_call(functools.partial(backward_kernel, chunk), grid=(heads,),...  23.4 us

profile of v1, /device:TPU:0, one launch (start us, length us, event | category | flops | bytes accessed | tf_op | source)
XLA Modules:
  0.0 105.3 jit_solution(5057691395576578476)
XLA Ops:
  0.6 80.6 %forward_chain.1 = (bf16[768,2048]{1,0:T(8,128)(2,1)}, bf16[768,2048]{1,0:T(8,128)(2,1)}, bf16[16,3,128,128]{3,2,1,0:T(8,128)(2,1)}, bf16[16,3,128,128]{3,2,1,0:T(8,128)(2,1)}, f32[16,128]{1,0:T(8,128)}) custom-call(bf16[768,2048]{1,0:T(8,128)(2,1)} %q_ref.1, bf16[768,2048]{1,0:T(8,128)(2,1)} %k_ref.1, bf16[768,2048]{1,0:T(8,128)(2,1)} %v_ref.1, ...), custom_call_target="tpu_custom_call" | custom-call | tf_op jit(solution)/shard_map/forward_chain/pallas_call | solution.py:398
  81.2 0.0 copy-start
  81.2 23.4 %backward_heads.1 = (bf16[768,2048]{1,0:T(8,128)(2,1)}, bf16[768,2048]{1,0:T(8,128)(2,1)}, bf16[768,2048]{1,0:T(8,128)(2,1)}, bf16[768,2048]{1,0:T(8,128)(2,1)}) custom-call(bf16[768,2048]{1,0:T(8,128)(2,1)} %q_ref.1, bf16[768,2048]{1,0:T(8,128)(2,1)} %k_ref.1, bf16[768,2048]{1,0:T(8,128)(2,1)} %v_ref.1, bf16[768,2048]{1,0:T(8,128)(2,1)} %get-tuple-element.14.grad_ref, ...), custom_call_target="tpu_custom_call" | custom-call | tf_op jit(solution)/shard_map/backward_heads/pallas_call | solution.py:423
  104.7 0.0 copy-done
  104.7 0.6 copy.12
Async XLA Ops:
  81.2 23.4 %copy-start = (f32[16,128]{1,0:T(8,128)S(1)}, f32[16,128]{1,0:T(8,128)}, u32[]{:S(2)}) copy-start(f32[16,128]{1,0:T(8,128)} %get-tuple-element.22) | copy-start | bytes 24580

commit v2 on v1

--- a/solution.py
+++ b/solution.py
@@ -153,12 +153,12 @@
 def main_kernel(
     n, peers, chunk,
     q_hbm, k_hbm, v_hbm, g_hbm, ld_ref, gain_ref,
-    grad_hbm, out_hbm, s_out, r_out, gg_out,
-    q, k, v, g, att, obuf, cum_ref, lc, state_in, sq_acc, in_acc,
+    q, k, v, g, att, obuf, r_out, cum_ref, gg_out,
+    s_out, lc, state_in, sq_acc, in_acc,
     stat_send, stat_recv, gain_send, gain_recv, inv_b, cen_b,
     lsend1, lrecv1, zsend1, zrecv1, xsend1, xrecv1,
     lsend2, lrecv2, zsend2, zrecv2, xsend2, xrecv2,
-    load_sem, store_sem, chain1_sem, chain2_sem, stat_sem, gain_sem,
+    load_sem, chain1_sem, chain2_sem, stat_sem, gain_sem,
 ):
     heads, tokens, _ = q.shape
     chunks = tokens // chunk
@@ -169,10 +169,6 @@
     def load(i, hbm, vmem, h):
         where = pl.ds(pl.multiple_of(h * DH, DH), DH)
         return pltpu.make_async_copy(hbm.at[:, where], vmem.at[h], load_sem.at[i, h])
-
-    def store(i, vmem, hbm, h):
-        where = pl.ds(pl.multiple_of(h * DH, DH), DH)
-        return pltpu.make_async_copy(vmem.at[h], hbm.at[:, where], store_sem.at[i, h])
 
     def load_kv(h):
         load(0, k_hbm, k, h).start()
@@ -307,8 +303,6 @@
             decay = total if j == chunks - 1 else decay + total
         backward.give(h, state, jnp.exp(decay))
         gain_send[pl.ds(h, 1), :] = gain_part
-        store(0, g, grad_hbm, h).start()
-        store(1, obuf, out_hbm, h).start()
 
     loop(heads, normalize)
 
@@ -319,7 +313,34 @@
         gain_copy(off, me).start()
     gain_recv[me] = gain_send[...]
 
-    loop(heads, lambda h: backward.step(h, state_in))
+    def gradients(h):
+        for j in range(chunks):
+            span = slice(j * chunk, (j + 1) * chunk)
+            row, column = cum_forms(cum_ref, h, j, chunk)
+            decay = decay_of(row, column)
+            queries, keys, values, grad = q[h, span], k[h, span], v[h, span], g[h, span]
+            weights = (mm(queries, keys, ABT) * decay).astype(BF16)
+            grad_weights = (mm(grad, values, ABT) * decay).astype(BF16)
+            q[h, span] = (
+                mm(grad_weights, keys, AB) + jnp.exp(column) * mm(grad, s_out[h, j], ABT)
+            ).astype(BF16)
+            att[h, span] = mm(grad_weights, queries, ATB)
+            g[h, span] = mm(weights, grad, ATB).astype(BF16)
+
+    back_lag = backward.row * 2 + 1
+
+    def overlap_back(i):
+        at = i - back_lag
+
+        @pl.when(jnp.logical_and(at >= 0, at < heads))
+        def _():
+            backward.step(at, state_in)
+
+        @pl.when(i < heads)
+        def _():
+            gradients(i)
+
+    loop(heads + n, overlap_back)
 
     def after(h):
         backward.take(h, state_in)
@@ -342,8 +363,6 @@
     def finish(h):
         forward.finish(h)
         backward.finish(h)
-        store(0, g, grad_hbm, h).wait()
-        store(1, obuf, out_hbm, h).wait()
 
     loop(heads, finish)
     for off in range(1, peers):
@@ -352,31 +371,43 @@
         gain_copy(off, me).wait_send()
 
 
-def backward_kernel(
-    chunk, q_ref, k_ref, v_ref, grad_ref, pass_ref, ld_ref, s_ref, r_ref,
-    out_ref, gq_ref, gk_ref, gv_ref, cum_ref,
+def last_kernel(
+    chunk, k, v, gq, gk, gv, out, after, cum_ref,
+    out_hbm, gq_hbm, gk_hbm, gv_hbm, k_stage, v_stage, store_sem,
 ):
-    h = pl.program_id(0)
-    tokens = q_ref.shape[0]
-
-    @pl.when(h == 0)
-    def _():
-        chunk_cumsum(ld_ref, cum_ref, chunk)
-
-    out_ref[...] = pass_ref[...]
-    for j in range(tokens // chunk):
-        span = slice(j * chunk, (j + 1) * chunk)
-        row, column = cum_forms(cum_ref, h, j, chunk)
-        decay = decay_of(row, column)
-        growth = jnp.exp(column)
-        tail = jnp.exp(column[chunk - 1 : chunk, :] - column)
-        q, k, v, grad = q_ref[span], k_ref[span], v_ref[span], grad_ref[span]
-        weights = (mm(q, k, ABT) * decay).astype(BF16)
-        grad_weights = (mm(grad, v, ABT) * decay).astype(BF16)
-        state, after = s_ref[0, j], r_ref[0, j]
-        gq_ref[span] = (mm(grad_weights, k, AB) + growth * mm(grad, state, ABT)).astype(BF16)
-        gk_ref[span] = (mm(grad_weights, q, ATB) + tail * mm(v, after, ABT)).astype(BF16)
-        gv_ref[span] = (mm(weights, grad, ATB) + tail * mm(k, after, AB)).astype(BF16)
+    heads, tokens, _ = k.shape
+
+    def store(i, vmem, hbm, h):
+        where = pl.ds(pl.multiple_of(h * DH, DH), DH)
+        return pltpu.make_async_copy(vmem.at[h], hbm.at[:, where], store_sem.at[i, h])
+
+    def copies(h):
+        return (
+            store(0, out, out_hbm, h), store(1, gq, gq_hbm, h),
+            store(2, k_stage, gk_hbm, h), store(3, v_stage, gv_hbm, h),
+        )
+
+    def one(h):
+        ready = copies(h)
+        ready[0].start()
+        ready[1].start()
+        for j in range(tokens // chunk):
+            span = slice(j * chunk, (j + 1) * chunk)
+            _, column = cum_forms(cum_ref, h, j, chunk)
+            tail = jnp.exp(column[chunk - 1 : chunk, :] - column)
+            k_stage[h, span] = (gk[h, span] + tail * mm(v[h, span], after[h, j], ABT)).astype(BF16)
+            v_stage[h, span] = (
+                gv[h, span].astype(F32) + tail * mm(k[h, span], after[h, j], AB)
+            ).astype(BF16)
+        ready[2].start()
+        ready[3].start()
+
+    def wait(h):
+        for copy in copies(h):
+            copy.wait()
+
+    loop(heads, one)
+    loop(heads, wait)
 
 
 def on_device(n, peers, queries, key_rows, value_rows, log_decay, norm_gain, grad_out):
@@ -395,40 +426,43 @@
         per_head(DH, DH), per_head(DH, DH), per_head(DH, DH),
     ]
     dma = pltpu.SemaphoreType.DMA
-    grad, out, state, after, grad_gain = pl.pallas_call(
+    by_head = lambda dtype: pltpu.VMEM((heads, tokens, DH), dtype)
+    *held, grad_gain = pl.pallas_call(
         functools.partial(main_kernel, n, peers, chunk),
-        out_shape=(rows, rows, states, states, jax.ShapeDtypeStruct((heads, DH), F32)),
+        out_shape=(
+            by_head(BF16), by_head(BF16), by_head(BF16), by_head(BF16), by_head(F32), by_head(BF16),
+            pltpu.VMEM((heads, chunks, DH, DH), BF16), pltpu.VMEM((heads, tokens), F32),
+            jax.ShapeDtypeStruct((heads, DH), F32),
+        ),
         in_specs=[anywhere] * 4 + [vmem] * 2,
-        out_specs=(anywhere, anywhere, vmem, vmem, vmem),
+        out_specs=(vmem,) * 9,
         scratch_shapes=[
-            per_head(tokens, DH, dtype=BF16), per_head(tokens, DH, dtype=BF16),
-            per_head(tokens, DH, dtype=BF16), per_head(tokens, DH, dtype=BF16),
-            per_head(tokens, DH), per_head(tokens, DH, dtype=BF16),
-            pltpu.VMEM((heads, tokens), F32), per_head(chunks, DH, DH), per_head(DH, DH),
+            per_head(chunks, DH, DH, dtype=BF16), per_head(chunks, DH, DH), per_head(DH, DH),
             pltpu.VMEM((tokens, DH), F32), pltpu.VMEM((tokens, DH), F32),
             pltpu.VMEM((8, tokens), F32), pltpu.VMEM((peers, 8, tokens), F32),
             pltpu.VMEM((heads, DH), F32), pltpu.VMEM((n, heads, DH), F32),
             pltpu.VMEM((tokens, DH), F32), pltpu.VMEM((tokens, DH), F32),
             *chain, *chain,
-            dma((4, heads)), dma((2, heads)), dma((6, heads)), dma((6, heads)),
+            dma((4, heads)), dma((6, heads)), dma((6, heads)),
             dma((2, peers)), dma((2, n)),
         ],
         compiler_params=pltpu.CompilerParams(
-            collective_id=0, has_side_effects=True, vmem_limit_bytes=60 * 1024 * 1024
+            collective_id=0, has_side_effects=True, vmem_limit_bytes=32 * 1024 * 1024
         ),
         name="forward_chain",
     )(queries, key_rows, value_rows, grad_out, log_decay, gain)
-    block = pl.BlockSpec((tokens, DH), lambda h: (0, h))
-    per_state = pl.BlockSpec((1, chunks, DH, DH), lambda h: (h, 0, 0, 0))
+    grad_q, key_held, value_held, grad_v, grad_k, out, after, cumulative = held
     out, grad_q, grad_k, grad_v = pl.pallas_call(
-        functools.partial(backward_kernel, chunk),
-        grid=(heads,),
+        functools.partial(last_kernel, chunk),
         out_shape=(rows,) * 4,
-        in_specs=[block] * 5 + [pl.BlockSpec((heads, tokens), lambda h: (0, 0)), per_state, per_state],
-        out_specs=(block,) * 4,
-        scratch_shapes=[pltpu.VMEM((heads, tokens), F32)],
-        name="backward_heads",
-    )(queries, key_rows, value_rows, grad, out, log_decay, state, after)
+        in_specs=[vmem] * 8,
+        out_specs=(anywhere,) * 4,
+        scratch_shapes=[
+            per_head(tokens, DH, dtype=BF16), per_head(tokens, DH, dtype=BF16), dma((4, heads)),
+        ],
+        compiler_params=pltpu.CompilerParams(vmem_limit_bytes=16 * 1024 * 1024),
+        name="last_terms",
+    )(key_held, value_held, grad_q, grad_k, grad_v, out, after, cumulative)
     return out, grad_q, grad_k, grad_v, grad_gain.reshape(width)
 
 

time: 106 us -> 93.1 us (0.88)
  Pallas kernels: 104 us -> 91.7 us
    pallas_call x1, Pallas kernels: 23.4 us -> 5.48 us  [on_device(): pl.pallas_call(functools.partial(last_kernel, chunk), out_shape=(rows,) *...]
    pallas_call x1, Pallas kernels: 80.6 us -> 86.2 us  [on_device(): pl.pallas_call(functools.partial(main_kernel, n, peers, chunk), out_shape...]
where the time goes in v2:
time: 93.1 us; the launch traced here: 92.9 us
  Pallas kernels  91.7 us (98%)
    pallas_call x1, Pallas kernels, on_device(): pl.pallas_call(functools.partial(main_kernel, n, peers, chunk), out_shape...  86.2 us
    pallas_call x1, Pallas kernels, on_device(): pl.pallas_call(functools.partial(last_kernel, chunk), out_shape=(rows,) *...  5.48 us

profile of v2, /device:TPU:0, one launch (start us, length us, event | category | flops | bytes accessed | tf_op | source)
XLA Modules:
  0.0 92.9 jit_solution(2203372175538669324)
XLA Ops:
  0.6 86.2 %forward_chain.1 = (bf16[16,768,128]{2,1,0:T(8,128)(2,1)S(1)}, bf16[16,768,128]{2,1,0:T(8,128)(2,1)S(1)}, bf16[16,768,128]{2,1,0:T(8,128)(2,1)S(1)}, bf16[16,768...) custom-call(bf16[768,2048]{1,0:T(8,128)(2,1)} %q_hbm.1, ...), custom_call_target="tpu_custom_call" | custom-call | tf_op jit(solution)/shard_map/forward_chain/pallas_call | solution.py:430
  86.8 0.0 copy-start
  86.8 5.5 %last_terms.1 = (bf16[768,2048]{1,0:T(8,128)(2,1)}, bf16[768,2048]{1,0:T(8,128)(2,1)}, bf16[768,2048]{1,0:T(8,128)(2,1)}, bf16[768,2048]{1,0:T(8,128)(2,1)}) custom-call(bf16[16,768,128]{2,1,0:T(8,128)(2,1)S(1)} %get-tuple-element.18.k, bf16[16,768,128]{2,1,0:T(8,128)(2,1)S(1)} %get-tuple-element.19.v, bf16[16,768,128]{2,1,0:T(8,128)(2,1)S(1)} %get-tuple-element.20.gq, ...), custom_call_target="tpu_custom_call" | custom-call | tf_op jit(solution)/shard_map/last_terms/pallas_call | solution.py:455
  92.3 0.0 copy-done
  92.3 0.6 copy.12
Async XLA Ops:
  86.8 5.5 %copy-start = (f32[16,128]{1,0:T(8,128)S(1)}, f32[16,128]{1,0:T(8,128)}, u32[]{:S(2)}) copy-start(f32[16,128]{1,0:T(8,128)} %get-tuple-element.30) | copy-start | bytes 24580

commit v3 on v2

--- a/solution.py
+++ b/solution.py
@@ -222,21 +222,6 @@
             weights = (scores * decay_of(row, column)).astype(BF16)
             att[h, span] = mm(weights, v[h, span], AB)
 
-    lag = forward.row * 2 + 1
-
-    def overlap(i):
-        @pl.when(i < heads)
-        def _():
-            intra(i)
-
-        at = i - lag
-
-        @pl.when(jnp.logical_and(at >= 0, at < heads))
-        def _():
-            forward.step(at, state_in)
-
-    loop(heads + n, overlap)
-
     sq_acc[...] = jnp.zeros_like(sq_acc)
     in_acc[...] = jnp.zeros_like(in_acc)
 
@@ -257,7 +242,26 @@
             if j < chunks - 1:
                 state = jnp.exp(column[chunk - 1 : chunk, :]) * state + lc[h, j]
 
-    loop(heads, inter)
+    lag = forward.row * 2 + 1
+
+    def overlap(i):
+        @pl.when(i < heads)
+        def _():
+            intra(i)
+
+        at = i - lag
+
+        @pl.when(jnp.logical_and(at >= 0, at < heads))
+        def _():
+            forward.step(at, state_in)
+
+        ready = at - 2
+
+        @pl.when(jnp.logical_and(ready >= 0, ready < heads))
+        def _():
+            inter(ready)
+
+    loop(heads + n + 2, overlap)
 
     ones = jnp.ones((8, DH), F32)
 

time: 93.1 us -> 108 us (1.16)
  Pallas kernels: 91.7 us -> 107 us
    pallas_call x1, Pallas kernels: 86.2 us -> 101 us  [on_device(): pl.pallas_call(functools.partial(main_kernel, n, peers, chunk), out_shape...]
where the time goes in v3:
time: 108 us
  Pallas kernels  107 us (99%)
    pallas_call x1, Pallas kernels, on_device(): pl.pallas_call(functools.partial(main_kernel, n, peers, chunk), out_shape...  101 us
    pallas_call x1, Pallas kernels, on_device(): pl.pallas_call(functools.partial(last_kernel, chunk), out_shape=(rows,) *...  5.48 us

profile of v3, /device:TPU:0, one launch (start us, length us, event | category | flops | bytes accessed | tf_op | source)
XLA Modules:
  0.0 108.1 jit_solution(4209414396137490862)
XLA Ops:
  0.6 101.3 %forward_chain.1 = (bf16[16,768,128]{2,1,0:T(8,128)(2,1)S(1)}, bf16[16,768,128]{2,1,0:T(8,128)(2,1)S(1)}, bf16[16,768,128]{2,1,0:T(8,128)(2,1)S(1)}, bf16[16,768...) custom-call(bf16[768,2048]{1,0:T(8,128)(2,1)} %q_hbm.1, ...), custom_call_target="tpu_custom_call" | custom-call | tf_op jit(solution)/shard_map/forward_chain/pallas_call | solution.py:434
  102.0 0.0 copy-start
  102.0 5.5 %last_terms.1 = (bf16[768,2048]{1,0:T(8,128)(2,1)}, bf16[768,2048]{1,0:T(8,128)(2,1)}, bf16[768,2048]{1,0:T(8,128)(2,1)}, bf16[768,2048]{1,0:T(8,128)(2,1)}) custom-call(bf16[16,768,128]{2,1,0:T(8,128)(2,1)S(1)} %get-tuple-element.18.k, bf16[16,768,128]{2,1,0:T(8,128)(2,1)S(1)} %get-tuple-element.19.v, bf16[16,768,128]{2,1,0:T(8,128)(2,1)S(1)} %get-tuple-element.20.gq, ...), custom_call_target="tpu_custom_call" | custom-call | tf_op jit(solution)/shard_map/last_terms/pallas_call | solution.py:459
  107.5 0.0 copy-done
  107.5 0.6 copy.12
Async XLA Ops:
  102.0 5.5 %copy-start = (f32[16,128]{1,0:T(8,128)S(1)}, f32[16,128]{1,0:T(8,128)}, u32[]{:S(2)}) copy-start(f32[16,128]{1,0:T(8,128)} %get-tuple-element.30) | copy-start | bytes 24580
